TPU v7x, 32 devices: a whole 2x2x4 slice. The times are simulated.
32 devices in a mesh: shard: 2 (over x), context: 4 (over y, core), tensor: 4 (over z).
Axes of the slice: x: 2, y: 2, z: 4, core: 2. Of those that a mesh axis runs over, the one named last changes fastest.
Arguments:
- tokens: bfloat16 [2, 2048, 2048], P('shard', 'context'), may hold values from -6 to 6
- block_order: int32 [2, 8], P('shard'), may hold values from 0 to 7, each once within a row
- w_query: bfloat16 [2048, 2048], P(('shard', 'context'), 'tensor'), may hold values from -0.5 to 0.5
- w_key: bfloat16 [2048, 512], P(('shard', 'context'), 'tensor'), may hold values from -0.5 to 0.5
- w_value: bfloat16 [2048, 512], P(('shard', 'context'), 'tensor'), may hold values from -0.125 to 0.125
- w_output: bfloat16 [2048, 2048], P('tensor', ('shard', 'context')), may hold values from -1.5 to 1.5
- w_gate: bfloat16 [2048, 8192], P(('shard', 'context'), 'tensor'), may hold values from -0.125 to 0.125
- w_up: bfloat16 [2048, 8192], P(('shard', 'context'), 'tensor'), may hold values from -0.125 to 0.125
- w_down: bfloat16 [8192, 2048], P('tensor', ('shard', 'context')), may hold values from -0.5 to 0.5
- norm_attn: bfloat16 [2048], P(('shard', 'context')), may hold values from 0.5 to 1.5
- norm_ffn: bfloat16 [2048], P(('shard', 'context')), may hold values from 0.5 to 1.5
- grad_out: bfloat16 [2, 2048, 2048], P('shard', 'context'), may hold values from -6 to 6
Outputs:
- layer_out: bfloat16 [2, 2048, 2048], P('shard', 'context')
- grad_tokens: float32 [2, 2048, 2048], P('shard', 'context')
- grad_w_query: float32 [2048, 2048], P(('shard', 'context'), 'tensor')
- grad_w_key: float32 [2048, 512], P(('shard', 'context'), 'tensor')
- grad_w_value: float32 [2048, 512], P(('shard', 'context'), 'tensor')
- grad_w_output: float32 [2048, 2048], P('tensor', ('shard', 'context'))
- grad_w_gate: float32 [2048, 8192], P(('shard', 'context'), 'tensor')
- grad_w_up: float32 [2048, 8192], P(('shard', 'context'), 'tensor')
- grad_w_down: float32 [8192, 2048], P('tensor', ('shard', 'context'))
- grad_norm_attn: float32 [2048], P(('shard', 'context'))
- grad_norm_ffn: float32 [2048], P(('shard', 'context'))
Inputs may be any that keep to these rules, and one draw needn't show every extreme that they name: Each row is a permutation of the 8 blocks of its sequence; stored block j of sequence s holds the tokens of block block_order[s, j].
All inputs are finite; a program needn't handle non-finite values.
Results may differ from a plain program's by a relative error of at most 0.015.
Values may be sent and summed in bfloat16 or wider, within the bound.
A program may use at most 192 MiB of HBM per device.

v0:
```python
import math
import jax
import jax.numpy as jnp
from jax import lax
from jax.sharding import PartitionSpec as P

HD = 64
BLK = 256
EPSILON = 1e-05
SCORE_SCALE = 0.015625
RESIDUAL_SCALE = 0.22
ROPE_BASE = 10000000.0
MASKED_SCORE = -1e30


def rope_tables(placed):
    half_dim = HD // 2
    inverse = jnp.exp(jnp.arange(half_dim, dtype=jnp.float32) * (-2.0 * math.log(ROPE_BASE) / HD))
    angles = placed.astype(jnp.float32)[:, None] * inverse[None, :]
    angles = jnp.concatenate([angles, angles], axis=1)
    return (jnp.cos(angles), jnp.sin(angles))


def rotate(values, cosine, sine):
    half_dim = values.shape[-1] // 2
    turned = jnp.concatenate([-values[..., half_dim:], values[..., :half_dim]], axis=-1)
    return values * cosine[:, None, :] + turned * sine[:, None, :]


def rms_norm(values, gain):
    return values * lax.rsqrt(jnp.mean(values * values, axis=-1, keepdims=True) + EPSILON) * gain


def stored_places(order_row, first, count):
    stored = first + jnp.arange(count, dtype=jnp.int32)
    picks = (stored // BLK)[:, None] == jnp.arange(order_row.shape[0], dtype=jnp.int32)[None, :]
    return jnp.sum(jnp.where(picks, order_row[None, :], 0), axis=1) * BLK + stored % BLK


def fetch_weights(w_query, w_key, w_value, w_output, w_gate, w_up, w_down, norm_attn, norm_ffn):
    return (
        lax.all_gather(w_query, ("shard", "context"), axis=0, tiled=True),
        lax.all_gather(w_key, ("shard", "context"), axis=0, tiled=True),
        lax.all_gather(w_value, ("shard", "context"), axis=0, tiled=True),
        lax.all_gather(w_output, ("shard", "context"), axis=1, tiled=True),
        lax.all_gather(w_gate, ("shard", "context"), axis=0, tiled=True),
        lax.all_gather(w_up, ("shard", "context"), axis=0, tiled=True),
        lax.all_gather(w_down, ("shard", "context"), axis=1, tiled=True),
        lax.all_gather(norm_attn, ("shard", "context"), axis=0, tiled=True),
        lax.all_gather(norm_ffn, ("shard", "context"), axis=0, tiled=True),
    )


def branch_total(partial_sum):
    return lax.psum(partial_sum, "tensor")


def norm_total(partial_sum):
    return lax.psum(partial_sum, "tensor")


def to_rows(items, seq_count, kv_count, group_size, local_len):
    head_dim = items.shape[-1]
    shaped = items.reshape(seq_count, kv_count, group_size, local_len, head_dim).transpose(
        0, 3, 1, 2, 4
    )
    return shaped.reshape(seq_count * local_len, kv_count * group_size * head_dim)


def from_rows(rows_in, seq_count, kv_count, group_size, local_len):
    shaped = rows_in.reshape(seq_count, local_len, kv_count, group_size, HD).transpose(
        0, 2, 3, 1, 4
    )
    return shaped.reshape(seq_count * kv_count, group_size * local_len, HD)


def softmax_rows(query_rows, key_rows, query_block, key_block):
    scores = SCORE_SCALE * jnp.einsum(
        "qd,kd->qk", query_rows, key_rows, preferred_element_type=jnp.float32
    )
    scores = jnp.where(key_block[None, :] <= query_block[:, None], scores, MASKED_SCORE)
    row_max = jnp.max(scores, axis=1, keepdims=True)
    exponent = jnp.exp(scores - row_max)
    return exponent / jnp.sum(exponent, axis=1, keepdims=True)


def attend_forward(packed, exact):
    query_rows, key_rows, value_rows, query_block, key_block = packed
    soft_weights = softmax_rows(query_rows, key_rows, query_block, key_block)
    rounded = soft_weights.astype(jnp.bfloat16)
    mixture = jnp.dot(rounded, value_rows, preferred_element_type=jnp.float32)
    if exact:
        remainder = (soft_weights - rounded.astype(jnp.float32)).astype(jnp.bfloat16)
        return (
            mixture,
            mixture + jnp.dot(remainder, value_rows, preferred_element_type=jnp.float32),
        )
    return (mixture, mixture)


def attend_backward(packed):
    query_rows, key_rows, value_rows, query_block, key_block, exact_rows, grad_rows = packed
    soft_weights = softmax_rows(query_rows, key_rows, query_block, key_block)
    grad_soft = jnp.einsum("qd,kd->qk", grad_rows, value_rows, preferred_element_type=jnp.float32)
    inner = jnp.sum(grad_rows.astype(jnp.float32) * exact_rows, axis=1, keepdims=True)
    grad_scores = (soft_weights * (grad_soft - inner)).astype(jnp.bfloat16)
    grad_query = SCORE_SCALE * jnp.dot(grad_scores, key_rows, preferred_element_type=jnp.float32)
    grad_key = SCORE_SCALE * jnp.einsum(
        "qk,qd->kd", grad_scores, query_rows, preferred_element_type=jnp.float32
    )
    grad_value = jnp.einsum(
        "qk,qd->kd",
        soft_weights.astype(jnp.bfloat16),
        grad_rows,
        preferred_element_type=jnp.float32,
    )
    return (grad_query, grad_key, grad_value)


def layer_pass(tokens_f, order, weight_set, exact):
    w_query, w_key, w_value, w_output, w_gate, w_up, w_down, norm_attn, norm_ffn = weight_set
    seq_count = order.shape[0]
    row_count = tokens_f.shape[0]
    local_len = row_count // seq_count
    full_len = local_len * lax.axis_size("context")
    first = lax.axis_index("context") * local_len
    q_places = jnp.stack([stored_places(order[0], first, local_len)])
    k_places = jnp.stack([stored_places(order[0], 0, full_len)])
    cosine, sine = rope_tables(q_places.reshape(-1))
    head_count = w_query.shape[1] // HD
    kv_count = w_key.shape[1] // HD
    group_size = head_count // kv_count
    normed = rms_norm(tokens_f, norm_attn.astype(jnp.float32)).astype(jnp.bfloat16)
    query_lin = jnp.dot(normed, w_query, preferred_element_type=jnp.float32)
    key_lin = jnp.dot(normed, w_key, preferred_element_type=jnp.float32)
    value_low = jnp.dot(normed, w_value, preferred_element_type=jnp.float32).astype(jnp.bfloat16)
    query_rot = rotate(query_lin.reshape(row_count, head_count, HD), cosine, sine).astype(
        jnp.bfloat16
    )
    key_rot = rotate(key_lin.reshape(row_count, kv_count, HD), cosine, sine).astype(jnp.bfloat16)
    key_all, value_all = (
        lax.all_gather(
            key_rot.reshape(seq_count, local_len, kv_count * HD), "context", axis=1, tiled=True
        ),
        lax.all_gather(
            value_low.reshape(seq_count, local_len, kv_count * HD), "context", axis=1, tiled=True
        ),
    )
    item_count = seq_count * kv_count
    query_items = from_rows(
        query_rot.reshape(row_count, head_count * HD), seq_count, kv_count, group_size, local_len
    )
    key_items = (
        key_all.reshape(seq_count, full_len, kv_count, HD)
        .transpose(0, 2, 1, 3)
        .reshape(item_count, full_len, HD)
    )
    value_items = (
        value_all.reshape(seq_count, full_len, kv_count, HD)
        .transpose(0, 2, 1, 3)
        .reshape(item_count, full_len, HD)
    )
    query_block = jnp.repeat(jnp.tile(q_places // BLK, (1, group_size)), kv_count, axis=0)
    key_block = jnp.repeat(k_places // BLK, kv_count, axis=0)
    mixture, exact_mix = lax.map(
        lambda packed: attend_forward(packed, exact),
        (query_items, key_items, value_items, query_block, key_block),
    )
    mixed_low = to_rows(mixture, seq_count, kv_count, group_size, local_len).astype(jnp.bfloat16)
    branch = branch_total(jnp.dot(mixed_low, w_output, preferred_element_type=jnp.float32))
    hidden = tokens_f + RESIDUAL_SCALE * branch
    normed_ffn = rms_norm(hidden, norm_ffn.astype(jnp.float32)).astype(jnp.bfloat16)
    gate_in = jnp.dot(normed_ffn, w_gate, preferred_element_type=jnp.float32)
    upward = jnp.dot(normed_ffn, w_up, preferred_element_type=jnp.float32)
    active = (jax.nn.silu(gate_in) * upward).astype(jnp.bfloat16)
    saved = (
        normed,
        cosine,
        sine,
        query_items,
        key_items,
        value_items,
        query_block,
        key_block,
        exact_mix,
        mixed_low,
        hidden,
        normed_ffn,
        gate_in,
        upward,
        active,
    )
    if exact:
        return (hidden, saved)
    layer_out = hidden + RESIDUAL_SCALE * branch_total(
        jnp.dot(active, w_down, preferred_element_type=jnp.float32)
    )
    return (layer_out, saved)


def local(
    tokens,
    block_order,
    w_query,
    w_key,
    w_value,
    w_output,
    w_gate,
    w_up,
    w_down,
    norm_attn,
    norm_ffn,
    grad_out,
):
    seq_count, local_len, width = tokens.shape
    row_count = seq_count * local_len
    tokens_f = tokens.reshape(row_count, width).astype(jnp.float32)
    gathered = fetch_weights(
        w_query, w_key, w_value, w_output, w_gate, w_up, w_down, norm_attn, norm_ffn
    )
    layer_out, unused_saved = layer_pass(tokens_f, block_order, gathered, False)
    again = fetch_weights(
        w_query, w_key, w_value, w_output, w_gate, w_up, w_down, norm_attn, norm_ffn
    )
    unused_hidden, saved = layer_pass(tokens_f, block_order, again, True)
    (
        normed,
        cosine,
        sine,
        query_items,
        key_items,
        value_items,
        query_block,
        key_block,
        exact_mix,
        mixed_low,
        hidden,
        normed_ffn,
        gate_in,
        upward,
        active,
    ) = saved
    (
        full_query,
        full_key,
        full_value,
        full_output,
        full_gate,
        full_up,
        full_down,
        full_norm_attn,
        full_norm_ffn,
    ) = again
    head_count = full_query.shape[1] // HD
    kv_count = full_key.shape[1] // HD
    group_size = head_count // kv_count
    full_len = key_items.shape[1]
    grad_rows = grad_out.reshape(row_count, width).astype(jnp.float32)
    d_ffn = (RESIDUAL_SCALE * grad_rows).astype(jnp.bfloat16)
    grad_down = jnp.einsum("rf,rd->fd", active, d_ffn, preferred_element_type=jnp.float32)
    d_active = jnp.einsum("rd,fd->rf", d_ffn, full_down, preferred_element_type=jnp.float32)
    unused_product, silu_pull = jax.vjp(
        lambda left, right: jax.nn.silu(left) * right, gate_in, upward
    )
    d_gate, d_upward = silu_pull(d_active)
    d_gate = d_gate.astype(jnp.bfloat16)
    d_upward = d_upward.astype(jnp.bfloat16)
    grad_gate = jnp.einsum("rd,rf->df", normed_ffn, d_gate, preferred_element_type=jnp.float32)
    grad_up = jnp.einsum("rd,rf->df", normed_ffn, d_upward, preferred_element_type=jnp.float32)
    d_normed_ffn = norm_total(
        jnp.einsum("rf,df->rd", d_gate, full_gate, preferred_element_type=jnp.float32)
        + jnp.einsum("rf,df->rd", d_upward, full_up, preferred_element_type=jnp.float32)
    )
    unused_norm, ffn_pull = jax.vjp(rms_norm, hidden, full_norm_ffn.astype(jnp.float32))
    d_hidden, grad_norm_ffn = ffn_pull(d_normed_ffn)
    d_hidden = grad_rows + d_hidden
    d_branch = (RESIDUAL_SCALE * d_hidden).astype(jnp.bfloat16)
    grad_output = jnp.einsum("rh,rd->hd", mixed_low, d_branch, preferred_element_type=jnp.float32)
    d_mixed = jnp.einsum(
        "rd,hd->rh", d_branch, full_output, preferred_element_type=jnp.float32
    ).astype(jnp.bfloat16)
    grad_items = from_rows(d_mixed, seq_count, kv_count, group_size, local_len)
    grad_query_items, grad_key_items, grad_value_items = lax.map(
        attend_backward,
        (query_items, key_items, value_items, query_block, key_block, exact_mix, grad_items),
    )
    key_grads = (
        grad_key_items.reshape(seq_count, kv_count, full_len, HD)
        .transpose(0, 2, 1, 3)
        .reshape(seq_count, full_len, kv_count * HD)
    )
    value_grads = (
        grad_value_items.reshape(seq_count, kv_count, full_len, HD)
        .transpose(0, 2, 1, 3)
        .reshape(seq_count, full_len, kv_count * HD)
    )
    key_local, value_local = (
        lax.psum_scatter(key_grads, "context", scatter_dimension=1, tiled=True),
        lax.psum_scatter(value_grads, "context", scatter_dimension=1, tiled=True),
    )
    query_back = to_rows(grad_query_items, seq_count, kv_count, group_size, local_len).reshape(
        row_count, head_count, HD
    )
    d_query = (
        rotate(query_back, cosine, -sine).reshape(row_count, head_count * HD).astype(jnp.bfloat16)
    )
    d_key = (
        rotate(key_local.reshape(row_count, kv_count, HD), cosine, -sine)
        .reshape(row_count, kv_count * HD)
        .astype(jnp.bfloat16)
    )
    d_value = value_local.reshape(row_count, kv_count * HD).astype(jnp.bfloat16)
    grad_query = jnp.einsum("rd,rh->dh", normed, d_query, preferred_element_type=jnp.float32)
    grad_key = jnp.einsum("rd,rh->dh", normed, d_key, preferred_element_type=jnp.float32)
    grad_value = jnp.einsum("rd,rh->dh", normed, d_value, preferred_element_type=jnp.float32)
    d_normed = norm_total(
        jnp.einsum("rh,dh->rd", d_query, full_query, preferred_element_type=jnp.float32)
        + jnp.einsum("rh,dh->rd", d_key, full_key, preferred_element_type=jnp.float32)
        + jnp.einsum("rh,dh->rd", d_value, full_value, preferred_element_type=jnp.float32)
    )
    unused_first, attn_pull = jax.vjp(rms_norm, tokens_f, full_norm_attn.astype(jnp.float32))
    d_tokens, grad_norm_attn = attn_pull(d_normed)
    grad_tokens = d_hidden + d_tokens
    reduced = (
        lax.psum_scatter(grad_query, ("shard", "context"), scatter_dimension=0, tiled=True),
        lax.psum_scatter(grad_key, ("shard", "context"), scatter_dimension=0, tiled=True),
        lax.psum_scatter(grad_value, ("shard", "context"), scatter_dimension=0, tiled=True),
        lax.psum_scatter(grad_output, ("shard", "context"), scatter_dimension=1, tiled=True),
        lax.psum_scatter(grad_gate, ("shard", "context"), scatter_dimension=0, tiled=True),
        lax.psum_scatter(grad_up, ("shard", "context"), scatter_dimension=0, tiled=True),
        lax.psum_scatter(grad_down, ("shard", "context"), scatter_dimension=1, tiled=True),
        lax.psum_scatter(grad_norm_attn, ("shard", "context"), scatter_dimension=0, tiled=True),
        lax.psum_scatter(grad_norm_ffn, ("shard", "context"), scatter_dimension=0, tiled=True),
    )
    return (
        layer_out.reshape(seq_count, local_len, width).astype(jnp.bfloat16),
        grad_tokens.reshape(seq_count, local_len, width),
        reduced[0],
        reduced[1],
        reduced[2],
        reduced[3],
        reduced[4],
        reduced[5],
        reduced[6],
        reduced[7],
        reduced[8],
    )


def solution(mesh):
    return jax.shard_map(
        local,
        mesh=mesh,
        in_specs=(
            P("shard", "context", None),
            P("shard", None),
            P(("shard", "context"), "tensor"),
            P(("shard", "context"), "tensor"),
            P(("shard", "context"), "tensor"),
            P("tensor", ("shard", "context")),
            P(("shard", "context"), "tensor"),
            P(("shard", "context"), "tensor"),
            P("tensor", ("shard", "context")),
            P(("shard", "context")),
            P(("shard", "context")),
            P("shard", "context", None),
        ),
        out_specs=(
            P("shard", "context", None),
            P("shard", "context", None),
            P(("shard", "context"), "tensor"),
            P(("shard", "context"), "tensor"),
            P(("shard", "context"), "tensor"),
            P("tensor", ("shard", "context")),
            P(("shard", "context"), "tensor"),
            P(("shard", "context"), "tensor"),
            P("tensor", ("shard", "context")),
            P(("shard", "context")),
            P(("shard", "context")),
        ),
        check_vma=False,
    )
```

profile of v0, /device:TPU:0, one launch (start us, length us, event | category | flops | bytes accessed | tf_op | source)
XLA Modules:
  0.0 1781.7 jit_solution(12693808725064753597)
XLA Ops:
  25.4 11.1 all_gather.46
  84.2 51.4 %while.37 = (s32[]{:T(128)}, bf16[2,2048,64]{1,2,0:T(8,128)(2,1)}, f32[2,2048,64]{1,2,0:T(8,128)}, s32[2,2048]{1,0:T(2,128)S(1)}, s32[2,2048]{1,0:T(2,128)S(1)},...) while((s32[]{:T(128)}, bf16[2,2048,64]{1,2,0:T(8,128)(2,1)}, ...), condition=%wide.region_13.14_spmd, body=%wide.region_10.13_spmd.sunk | while | flops 1690431488 | bytes 184675568 | solution.py:165
  156.3 26.2 %while.36 = (s32[]{:T(128)}, bf16[2,2048,64]{1,2,0:T(8,128)(2,1)}, s32[2,2048]{1,0:T(2,128)S(1)}, s32[2,2048]{1,0:T(2,128)S(1)}, bf16[2,2048,64]{2,1,0:T(8,128)(...) while((s32[]{:T(128)}, bf16[2,2048,64]{1,2,0:T(8,128)(2,1)}, ...), condition=%wide.region_6.7_spmd, body=%wide.region_3.6_spmd.sunk | while | flops 1136652288 | bytes 56748184 | solution.py:165
  192.3 108.3 %all-reduce.9.cloned.1.call-done = f32[512,2048]{1,0:T(8,128)} async-done(((f32[512,2048]{1,0:T(8,128)}), f32[512,2048]{1,0:T(8,128)}) %all-reduce.9.cloned.1.call-update) | async-done | bytes 4194320 | tf_op jit(solution)/shard_map/psum | solution.py:55
  306.4 49.2 %all-gather.13.cloned.1.call-done = bf16[2048,2048]{1,0:T(8,128)(2,1)} async-done(((bf16[256,2048]{1,0:T(8,128)(2,1)}), bf16[2048,2048]{1,0:T(8,128)(2,1)}) %all-gather.13.cloned.1.call-update) | async-done | bytes 8388624 | tf_op jit(solution)/shard_map/all_gather | solution.py:46
  366.1 45.5 %all-gather.15.cloned.1.call-done = bf16[2048,2048]{1,0:T(8,128)(2,1)} async-done(((bf16[256,2048]{1,0:T(8,128)(2,1)}), bf16[2048,2048]{1,0:T(8,128)(2,1)}) %all-gather.15.cloned.1.call-update) | async-done | bytes 8388624 | tf_op jit(solution)/shard_map/all_gather | solution.py:47
  422.1 47.1 %all-gather.17.cloned.1.call-done = bf16[2048,2048]{1,0:T(8,128)(2,1)} async-done(((bf16[2048,256]{1,0:T(8,128)(2,1)}), bf16[2048,2048]{1,0:T(8,128)(2,1)}) %all-gather.17.cloned.1.call-update) | async-done | bytes 8388624 | tf_op jit(solution)/shard_map/all_gather | solution.py:48
  469.2 12.3 multiply_convert_fusion.3
  481.6 11.1 fusion.176
  500.8 291.0 %all-reduce.13.cloned.1.call-done = (f32[512,2048]{1,0:T(8,128)}, f32[512,2048]{1,0:T(8,128)}) async-done(((f32[512,2048]{1,0:T(8,128)}, f32[512,2048]{1,0:T(8,128)}), (f32[512,2048]{1,0:T(8,128)}, f32[512,2048]{1,0:T(8,128)})) %all-reduce.13.cloned.1.call-update) | async-done | bytes 8388624 | tf_op jit(solution)/shard_map/psum | solution.py:59
  812.1 65.3 %while.38 = (s32[]{:T(128)}, f32[2,2048,64]{1,2,0:T(8,128)}, f32[2,2048,64]{1,2,0:T(8,128)}, f32[2,2048,64]{1,2,0:T(8,128)}, s32[2,2048]{1,0:T(2,128)S(1)}, /*in...) while((s32[]{:T(128)}, f32[2,2048,64]{1,2,0:T(8,128)}, ...), condition=%wide.region_22.23_spmd, body=%wide.region_18.22_spmd.sunk | while | flops 2781472768 | bytes 199144912 | solution.py:283
  878.2 10.8 fusion.171
  889.0 18.3 %fusion.172 = f32[512,2048]{1,0:T(8,128)} fusion(bf16[2048,2048]{1,0:T(8,128)(2,1)} %all-gather.17.cloned.1.call-done, f32[512,2048]{1,0:T(8,128)} %fusion.171, bf16[512,2048]{1,0:T(8,128)(2,1)S(1)} %copy-done.38, bf16[2048,2048]{1,0:T(8,128)(2,1)} %all-gather.15.cloned.1.call-done), kind=kOutput, calls=%fused_computation.249 | convolution fusion | flops 8596226048 | bytes 27262976 | tf_op jit(solution)/shard_map/dot_general | solution.py:196
  952.8 14.6 fusion.97
  967.7 12.6 fusion.180
  980.4 12.6 fusion.179
  994.9 231.0 %all-reduce.11.cloned.1.call-done = (f32[512,2048]{1,0:T(8,128)}, f32[512,2048]{1,0:T(8,128)}) async-done(((f32[512,2048]{1,0:T(8,128)}, f32[512,2048]{1,0:T(8,128)}), (f32[512,2048]{1,0:T(8,128)}, f32[512,2048]{1,0:T(8,128)})) %all-reduce.11.cloned.1.call-update) | async-done | bytes 8388624 | tf_op jit(solution)/shard_map/psum | solution.py:55
  1229.4 24.1 %all-reduce.2 = (f32[2048]{0:T(1024)S(1)}, f32[2048]{0:T(1024)S(1)}) all-reduce(f32[2048]{0:T(1024)S(1)} %get-tuple-element.235, f32[2048]{0:T(1024)S(1)} %copy-done.51), channel_id=12, replica_groups=mesh['shard'=2,'context'=4,'tensor'=4] {'shard','context'}, use_global_device_ids=true, to_apply=%region_35.36.clone | all-reduce | flops 4096 | bytes 32768
  1264.7 39.6 %reduce-scatter.18.cloned.1.call-done = f32[256,128]{1,0:T(8,128)} async-done(((f32[2048,128]{1,0:T(8,128)}), f32[256,128]{1,0:T(8,128)}) %reduce-scatter.18.cloned.1.call-update) | async-done | bytes 131088 | tf_op jit(solution)/shard_map/reduce_scatter | solution.py:327
  1304.3 55.0 %reduce-scatter.20.cloned.1.call-done = f32[512,256]{1,0:T(8,128)} async-done(((f32[512,2048]{1,0:T(8,128)}), f32[512,256]{1,0:T(8,128)}) %reduce-scatter.20.cloned.1.call-update) | async-done | bytes 524304 | tf_op jit(solution)/shard_map/reduce_scatter | solution.py:328
  1359.3 55.0 %reduce-scatter.14.cloned.1.call-done = f32[256,512]{1,0:T(8,128)} async-done(((f32[2048,512]{1,0:T(8,128)}), f32[256,512]{1,0:T(8,128)}) %reduce-scatter.14.cloned.1.call-update) | async-done | bytes 524304 | tf_op jit(solution)/shard_map/reduce_scatter | solution.py:325
  1414.3 120.0 %reduce-scatter.26.cloned.1.call-done = f32[2048,256]{1,0:T(8,128)} async-done(((f32[2048,2048]{1,0:T(8,128)}), f32[2048,256]{1,0:T(8,128)}) %reduce-scatter.26.cloned.1.call-update) | async-done | bytes 2097168 | tf_op jit(solution)/shard_map/reduce_scatter | solution.py:331
  1534.3 120.2 %reduce-scatter.24.cloned.1.call-done = f32[256,2048]{1,0:T(8,128)} async-done(((f32[2048,2048]{1,0:T(8,128)}), f32[256,2048]{1,0:T(8,128)}) %reduce-scatter.24.cloned.1.call-update) | async-done | bytes 2097168 | tf_op jit(solution)/shard_map/reduce_scatter | solution.py:330
  1654.5 120.2 %reduce-scatter.22.cloned.1.call-done = f32[256,2048]{1,0:T(8,128)} async-done(((f32[2048,2048]{1,0:T(8,128)}), f32[256,2048]{1,0:T(8,128)}) %reduce-scatter.22.cloned.1.call-update) | async-done | bytes 2097168 | tf_op jit(solution)/shard_map/reduce_scatter | solution.py:329
  (317 shorter events, 354.7 us)
Async XLA Ops:
  7.2 65.9 %all-gather.9.cloned.1.call-start = ((), (), s32[]{:S(2)}) async-start(), calls=%async_computation.9 | async-start | bytes 2359296 | tf_op jit(solution)/shard_map/all_gather | solution.py:42
  7.9 131.8 %all-gather.11.cloned.1.call-start = ((), (), s32[]{:S(2)}) async-start(), calls=%async_computation.10 | async-start | bytes 2359296 | tf_op jit(solution)/shard_map/all_gather | solution.py:45
  8.7 291.9 %all-reduce.9.cloned.1.call-start = ((), (), s32[]{:S(2)}) async-start(), calls=%async_computation.14 | async-start | bytes 8388608 | tf_op jit(solution)/shard_map/psum | solution.py:55
  12.4 65.0 %copy-start.49 = (f32[512]{0:T(512)}, f32[512]{0:T(512)S(1)}, u32[]{:S(2)}) copy-start(f32[512]{0:T(512)S(1)} %fusion.153) | copy-start | bytes 6148
  23.6 53.8 %copy-start.44 = (f32[8,1,256]{2,1,0:T(1,128)}, f32[8,1,256]{2,1,0:T(1,128)S(1)}, u32[]{:S(2)}) copy-start(f32[8,1,256]{2,1,0:T(1,128)S(1)} %convert_element_type.206) | copy-start | bytes 24580
  25.4 55.1 %copy-start.22 = (f32[512,64]{0,1:T(8,128)}, f32[512,64]{0,1:T(8,128)S(1)}, u32[]{:S(2)}) copy-start(f32[512,64]{0,1:T(8,128)S(1)} %get-tuple-element.334) | copy-start | bytes 393220
  144.8 210.8 %all-gather.13.cloned.1.call-start = ((), (), s32[]{:S(2)}) async-start(), calls=%async_computation.11 | async-start | bytes 9437184 | tf_op jit(solution)/shard_map/all_gather | solution.py:46
  145.4 266.2 %all-gather.15.cloned.1.call-start = ((), (), s32[]{:S(2)}) async-start(), calls=%async_computation.12 | async-start | bytes 9437184 | tf_op jit(solution)/shard_map/all_gather | solution.py:47
  146.0 323.2 %all-gather.17.cloned.1.call-start = ((), (), s32[]{:S(2)}) async-start(), calls=%async_computation.13 | async-start | bytes 9437184 | tf_op jit(solution)/shard_map/all_gather | solution.py:48
  146.6 645.2 %all-reduce.13.cloned.1.call-start = ((), (), s32[]{:S(2)}) async-start(), calls=%async_computation.25 | async-start | bytes 16777216 | tf_op jit(solution)/shard_map/psum | solution.py:59
  186.1 114.5 %copy-start.3 = (bf16[1,512,2048]{2,1,0:T(8,128)(2,1)S(1)}, bf16[1,512,2048]{2,1,0:T(8,128)(2,1)}, u32[]{:S(2)}) copy-start(bf16[1,512,2048]{2,1,0:T(8,128)(2,1)} %param.18) | copy-start | bytes 6291460
  192.3 111.4 %copy-start.47 = (f32[8,1,256]{2,1,0:T(1,128)S(1)}, f32[8,1,256]{2,1,0:T(1,128)}, u32[]{:S(2)}) copy-start(f32[8,1,256]{2,1,0:T(1,128)} %convert_element_type.207) | copy-start | bytes 24580
  500.7 413.1 %reduce-scatter.10.cloned.1.call-start = ((), (), s32[]{:S(2)}) async-start(), calls=%async_computation.15 | async-start | bytes 1310720 | tf_op jit(solution)/shard_map/reduce_scatter | solution.py:298
  877.4 51.3 %reduce-scatter.12.cloned.1.call-start = ((), (), s32[]{:S(2)}) async-start(), calls=%async_computation.16 | async-start | bytes 1310720 | tf_op jit(solution)/shard_map/reduce_scatter | solution.py:299
  878.1 347.8 %all-reduce.11.cloned.1.call-start = ((), (), s32[]{:S(2)}) async-start(), calls=%async_computation.24 | async-start | bytes 16777216 | tf_op jit(solution)/shard_map/psum | solution.py:55
  934.9 329.7 %reduce-scatter.16.cloned.1.call-start = ((), (), s32[]{:S(2)}) async-start(), calls=%async_computation.18 | async-start | bytes 1179648 | tf_op jit(solution)/shard_map/reduce_scatter | solution.py:326
  938.6 365.7 %reduce-scatter.18.cloned.1.call-start = ((), (), s32[]{:S(2)}) async-start(), calls=%async_computation.19 | async-start | bytes 1179648 | tf_op jit(solution)/shard_map/reduce_scatter | solution.py:327
  940.6 418.7 %reduce-scatter.20.cloned.1.call-start = ((), (), s32[]{:S(2)}) async-start(), calls=%async_computation.20 | async-start | bytes 4718592 | tf_op jit(solution)/shard_map/reduce_scatter | solution.py:328
  946.3 468.0 %reduce-scatter.14.cloned.1.call-start = ((), (), s32[]{:S(2)}) async-start(), calls=%async_computation.17 | async-start | bytes 4718592 | tf_op jit(solution)/shard_map/reduce_scatter | solution.py:325
  952.7 581.6 %reduce-scatter.26.cloned.1.call-start = ((), (), s32[]{:S(2)}) async-start(), calls=%async_computation.23 | async-start | bytes 18874368 | tf_op jit(solution)/shard_map/reduce_scatter | solution.py:331
  967.4 687.1 %reduce-scatter.24.cloned.1.call-start = ((), (), s32[]{:S(2)}) async-start(), calls=%async_computation.22 | async-start | bytes 18874368 | tf_op jit(solution)/shard_map/reduce_scatter | solution.py:330
  980.4 794.4 %reduce-scatter.22.cloned.1.call-start = ((), (), s32[]{:S(2)}) async-start(), calls=%async_computation.21 | async-start | bytes 18874368 | tf_op jit(solution)/shard_map/reduce_scatter | solution.py:329
  993.0 236.4 %copy-start.51 = (f32[2048]{0:T(1024)S(1)}, f32[2048]{0:T(1024)}, u32[]{:S(2)}) copy-start(f32[2048]{0:T(1024)} %get-tuple-element.233) | copy-start | bytes 24580
  993.1 261.7 %copy-start.53 = (f32[512]{0:T(512)S(1)}, f32[512]{0:T(512)}, u32[]{:S(2)}) copy-start(f32[512]{0:T(512)} %copy-done.52) | copy-start | bytes 6148
  (69 other events, 407.8 us)
Sparse Core Ops, SparseCore 0:
  9.9 31.1 all-gather.8
  43.0 31.8 all-gather.10
  144.9 155.5 all-reduce.8
  302.3 53.2 all-gather.12
  357.3 54.2 all-gather.14
  413.3 55.8 all-gather.16
  500.8 290.8 all-reduce.12
  877.5 23.7 reduce-scatter.9
  903.8 24.7 reduce-scatter.11
  935.0 290.8 all-reduce.10
  1229.7 34.9 reduce-scatter.15
  1268.3 35.9 reduce-scatter.17
  1308.2 51.0 reduce-scatter.19
  1363.1 51.1 reduce-scatter.13
  1418.3 115.9 reduce-scatter.25
  1538.3 116.1 reduce-scatter.23
  1658.5 116.1 reduce-scatter.21
where the time goes:
time: 1790 us; the launch traced here: 1780 us
  waiting for transfers between devices  1300 us (73%)
  matrix products  234 us (13%)
  other arithmetic  89.3 us (5%)
  blocking collectives  82.9 us (5%)
  local copies, waits for them, and re-layouts  61.1 us (3%)
    psum x2, waiting for transfers between devices, branch_total(): return lax.psum(partial_sum, 'tensor')  339 us
    psum x1, waiting for transfers between devices, norm_total(): return lax.psum(partial_sum, 'tensor')  291 us
    reduce_scatter x1, waiting for transfers between devices, local(): lax.psum_scatter(grad_up, ('shard', 'context'), scatter_dimension=0, tile...  120 us
    reduce_scatter x1, waiting for transfers between devices, local(): lax.psum_scatter(grad_gate, ('shard', 'context'), scatter_dimension=0, ti...  120 us
    reduce_scatter x1, waiting for transfers between devices, local(): lax.psum_scatter(grad_down, ('shard', 'context'), scatter_dimension=1, ti...  120 us
    reduce_scatter x1, waiting for transfers between devices, local(): lax.psum_scatter(grad_output, ('shard', 'context'), scatter_dimension=1,...  55 us
    reduce_scatter x1, waiting for transfers between devices, local(): lax.psum_scatter(grad_query, ('shard', 'context'), scatter_dimension=0, t...  55 us
    all_gather x1, waiting for transfers between devices, fetch_weights(): lax.all_gather(w_gate, ('shard', 'context'), axis=0, tiled=True)  49.2 us
  transfers between devices with their start and end apart: 17, of which 14 were waited for; matrix products, arithmetic and copies ran while one was open for 13% of the time, Pallas kernels for 0%

commit v1 on v0

--- a/solution.py
+++ b/solution.py
@@ -52,7 +52,11 @@
 
 
 def branch_total(partial_sum):
-    return lax.psum(partial_sum, "tensor")
+
+    def connect_lane_now(vec):
+        return jnp.sum(lax.all_gather(vec, axis_name="tensor"), axis=0)
+
+    return connect_lane_now(partial_sum)
 
 
 def norm_total(partial_sum):

time: 1790 us -> 2190 us (1.22)
  waiting for transfers between devices: 1300 us -> 1660 us
  other arithmetic: 89.3 us -> 124 us
    all_gather x0 -> x3, waiting for transfers between devices: none -> 749 us  [connect_lane_now(): return jnp.sum(lax.all_gather(vec, axis_name='tensor'), axis=0)]
    psum x2 -> x0, waiting for transfers between devices: 339 us -> none  [branch_total(): return lax.psum(partial_sum, 'tensor')]
    psum x1 -> x2, waiting for transfers between devices: 291 us -> 211 us  [norm_total(): return lax.psum(partial_sum, 'tensor')]
    reduce_sum x0 -> x3, other arithmetic: none -> 30.7 us  [connect_lane_now(): return jnp.sum(lax.all_gather(vec, axis_name='tensor'), axis=0)]
  transfers between devices with their start and end apart: 17 -> 19, of which waited for: 14 -> 17; matrix products, arithmetic and copies ran while one was open for 13% -> 14% of each run, Pallas kernels for 0% -> 0%
where the time goes in v1:
time: 2190 us; the launch traced here: 2180 us
  waiting for transfers between devices  1660 us (76%)
  matrix products  233 us (11%)
  other arithmetic  124 us (6%)
  blocking collectives  83.9 us (4%)
  local copies, waits for them, and re-layouts  60.9 us (3%)
    all_gather x3, waiting for transfers between devices, connect_lane_now(): return jnp.sum(lax.all_gather(vec, axis_name='tensor'), axis=0)  749 us
    psum x2, waiting for transfers between devices, norm_total(): return lax.psum(partial_sum, 'tensor')  211 us
    reduce_scatter x1, waiting for transfers between devices, local(): lax.psum_scatter(grad_gate, ('shard', 'context'), scatter_dimension=0, ti...  120 us
    reduce_scatter x1, waiting for transfers between devices, local(): lax.psum_scatter(grad_up, ('shard', 'context'), scatter_dimension=0, tile...  120 us
    reduce_scatter x1, waiting for transfers between devices, local(): lax.psum_scatter(grad_down, ('shard', 'context'), scatter_dimension=1, ti...  120 us
    reduce_scatter x1, waiting for transfers between devices, local(): lax.psum_scatter(grad_query, ('shard', 'context'), scatter_dimension=0, t...  55 us
    reduce_scatter x1, waiting for transfers between devices, local(): lax.psum_scatter(grad_output, ('shard', 'context'), scatter_dimension=1,...  54.9 us
    all_gather x1, waiting for transfers between devices, fetch_weights(): lax.all_gather(w_down, ('shard', 'context'), axis=1, tiled=True)  47.1 us
  transfers between devices with their start and end apart: 19, of which 17 were waited for; matrix products, arithmetic and copies ran while one was open for 14% of the time, Pallas kernels for 0%

profile of v1, /device:TPU:0, one launch (start us, length us, event | category | flops | bytes accessed | tf_op | source)
XLA Modules:
  0.0 2184.2 jit_solution(2433461671763799129)
XLA Ops:
  84.1 51.4 %while.37 = (s32[]{:T(128)}, bf16[2,2048,64]{1,2,0:T(8,128)(2,1)}, f32[2,2048,64]{1,2,0:T(8,128)}, s32[2,2048]{1,0:T(2,128)S(1)}, s32[2,2048]{1,0:T(2,128)S(1)},...) while((s32[]{:T(128)}, bf16[2,2048,64]{1,2,0:T(8,128)(2,1)}, ...), condition=%wide.region_13.14_spmd, body=%wide.region_10.13_spmd.sunk | while | flops 1690431488 | bytes 184675568 | solution.py:169
  146.5 25.9 %while.36 = (s32[]{:T(128)}, bf16[2,2048,64]{1,2,0:T(8,128)(2,1)}, s32[2,2048]{1,0:T(2,128)S(1)}, s32[2,2048]{1,0:T(2,128)S(1)}, bf16[2,2048,64]{2,1,0:T(8,128)(...) while((s32[]{:T(128)}, bf16[2,2048,64]{1,2,0:T(8,128)(2,1)}, ...), condition=%wide.region_6.7_spmd, body=%wide.region_3.6_spmd.sunk | while | flops 1136652288 | bytes 56748184 | solution.py:169
  190.7 241.5 %all-gather.29.cloned.1.call-done = f32[2048,2048]{1,0:T(8,128)} async-done(((f32[512,2048]{1,0:T(8,128)}), f32[2048,2048]{1,0:T(8,128)}) %all-gather.29.cloned.1.call-update) | async-done | bytes 16777232 | tf_op jit(solution)/shard_map/all_gather | solution.py:57
  448.4 38.0 %all-gather.19.cloned.1.call-done = bf16[2048,2048]{1,0:T(8,128)(2,1)} async-done(((bf16[256,2048]{1,0:T(8,128)(2,1)}), bf16[2048,2048]{1,0:T(8,128)(2,1)}) %all-gather.19.cloned.1.call-update) | async-done | bytes 8388624 | tf_op jit(solution)/shard_map/all_gather | solution.py:46
  497.0 45.5 %all-gather.21.cloned.1.call-done = bf16[2048,2048]{1,0:T(8,128)(2,1)} async-done(((bf16[256,2048]{1,0:T(8,128)(2,1)}), bf16[2048,2048]{1,0:T(8,128)(2,1)}) %all-gather.21.cloned.1.call-update) | async-done | bytes 8388624 | tf_op jit(solution)/shard_map/all_gather | solution.py:47
  553.0 47.1 %all-gather.23.cloned.1.call-done = bf16[2048,2048]{1,0:T(8,128)(2,1)} async-done(((bf16[2048,256]{1,0:T(8,128)(2,1)}), bf16[2048,2048]{1,0:T(8,128)(2,1)}) %all-gather.23.cloned.1.call-update) | async-done | bytes 8388624 | tf_op jit(solution)/shard_map/all_gather | solution.py:48
  632.3 256.1 %all-gather.25.cloned.1.call-done = f32[2048,2048]{1,0:T(8,128)} async-done(((f32[512,2048]{1,0:T(8,128)}), f32[2048,2048]{1,0:T(8,128)}) %all-gather.25.cloned.1.call-update) | async-done | bytes 16777232 | tf_op jit(solution)/shard_map/all_gather | solution.py:57
  898.7 145.3 %all-reduce.6.cloned.1.call-done = f32[512,2048]{1,0:T(8,128)} async-done(((f32[512,2048]{1,0:T(8,128)}), f32[512,2048]{1,0:T(8,128)}) %all-reduce.6.cloned.1.call-update) | async-done | bytes 4194320 | tf_op jit(solution)/shard_map/psum | solution.py:63
  1064.4 65.3 %while.38 = (s32[]{:T(128)}, f32[2,2048,64]{1,2,0:T(8,128)}, f32[2,2048,64]{1,2,0:T(8,128)}, f32[2,2048,64]{1,2,0:T(8,128)}, s32[2,2048]{1,0:T(2,128)S(1)}, /*in...) while((s32[]{:T(128)}, f32[2,2048,64]{1,2,0:T(8,128)}, ...), condition=%wide.region_22.23_spmd, body=%wide.region_18.22_spmd.sunk | while | flops 2781472768 | bytes 199144912 | solution.py:287
  1137.9 15.6 reduce-scatter.10.cloned.1.call-done
  1158.5 22.2 %reduce-scatter.12.cloned.1.call-done = f32[1,512,128]{1,2,0:T(8,128)} async-done(((f32[1,2048,128]{1,2,0:T(8,128)}), f32[1,512,128]{1,2,0:T(8,128)}) %reduce-scatter.12.cloned.1.call-update) | async-done | bytes 262160 | tf_op jit(solution)/shard_map/reduce_scatter | solution.py:303
  1198.1 18.1 fusion.173
  1233.9 14.6 fusion.98
  1261.4 13.4 fusion.180
  1276.7 65.6 %all-reduce.8.cloned.1.call-done = f32[512,2048]{1,0:T(8,128)} async-done(((f32[512,2048]{1,0:T(8,128)}), f32[512,2048]{1,0:T(8,128)}) %all-reduce.8.cloned.1.call-update) | async-done | bytes 4194320 | tf_op jit(solution)/shard_map/psum | solution.py:63
  1345.8 24.6 %all-reduce.2 = (f32[2048]{0:T(1024)S(1)}, f32[2048]{0:T(1024)S(1)}) all-reduce(f32[2048]{0:T(1024)S(1)} %get-tuple-element.235, f32[2048]{0:T(1024)S(1)} %copy-done.48), channel_id=15, replica_groups=mesh['shard'=2,'context'=4,'tensor'=4] {'shard','context'}, use_global_device_ids=true, to_apply=%region_35.36.clone | all-reduce | flops 4096 | bytes 32768
  1378.3 251.2 %all-gather.27.cloned.1.call-done = f32[2048,2048]{1,0:T(8,128)} async-done(((f32[512,2048]{1,0:T(8,128)}), f32[2048,2048]{1,0:T(8,128)}) %all-gather.27.cloned.1.call-update) | async-done | bytes 16777232 | tf_op jit(solution)/shard_map/all_gather | solution.py:57
  1645.8 21.6 reduce-scatter.16.cloned.1.call-done
  1667.4 39.6 %reduce-scatter.18.cloned.1.call-done = f32[256,128]{1,0:T(8,128)} async-done(((f32[2048,128]{1,0:T(8,128)}), f32[256,128]{1,0:T(8,128)}) %reduce-scatter.18.cloned.1.call-update) | async-done | bytes 131088 | tf_op jit(solution)/shard_map/reduce_scatter | solution.py:331
  1707.0 54.9 %reduce-scatter.20.cloned.1.call-done = f32[512,256]{1,0:T(8,128)} async-done(((f32[512,2048]{1,0:T(8,128)}), f32[512,256]{1,0:T(8,128)}) %reduce-scatter.20.cloned.1.call-update) | async-done | bytes 524304 | tf_op jit(solution)/shard_map/reduce_scatter | solution.py:332
  1761.9 55.0 %reduce-scatter.14.cloned.1.call-done = f32[256,512]{1,0:T(8,128)} async-done(((f32[2048,512]{1,0:T(8,128)}), f32[256,512]{1,0:T(8,128)}) %reduce-scatter.14.cloned.1.call-update) | async-done | bytes 524304 | tf_op jit(solution)/shard_map/reduce_scatter | solution.py:329
  1816.8 120.0 %reduce-scatter.26.cloned.1.call-done = f32[2048,256]{1,0:T(8,128)} async-done(((f32[2048,2048]{1,0:T(8,128)}), f32[2048,256]{1,0:T(8,128)}) %reduce-scatter.26.cloned.1.call-update) | async-done | bytes 2097168 | tf_op jit(solution)/shard_map/reduce_scatter | solution.py:335
  1936.9 120.2 %reduce-scatter.24.cloned.1.call-done = f32[256,2048]{1,0:T(8,128)} async-done(((f32[2048,2048]{1,0:T(8,128)}), f32[256,2048]{1,0:T(8,128)}) %reduce-scatter.24.cloned.1.call-update) | async-done | bytes 2097168 | tf_op jit(solution)/shard_map/reduce_scatter | solution.py:334
  2057.1 120.4 %reduce-scatter.22.cloned.1.call-done = f32[256,2048]{1,0:T(8,128)} async-done(((f32[2048,2048]{1,0:T(8,128)}), f32[256,2048]{1,0:T(8,128)}) %reduce-scatter.22.cloned.1.call-update) | async-done | bytes 2097168 | tf_op jit(solution)/shard_map/reduce_scatter | solution.py:333
  (321 shorter events, 436.6 us)
Async XLA Ops:
  7.2 65.9 %all-gather.15.cloned.1.call-start = ((), (), s32[]{:S(2)}) async-start(), calls=%async_computation.9 | async-start | bytes 2359296 | tf_op jit(solution)/shard_map/all_gather | solution.py:42
  7.9 131.7 %all-gather.17.cloned.1.call-start = ((), (), s32[]{:S(2)}) async-start(), calls=%async_computation.10 | async-start | bytes 2359296 | tf_op jit(solution)/shard_map/all_gather | solution.py:45
  8.7 423.6 %all-gather.29.cloned.1.call-start = ((), (), s32[]{:S(2)}) async-start(), calls=%async_computation.27 | async-start | bytes 20971520 | tf_op jit(solution)/shard_map/all_gather | solution.py:57
  12.4 64.9 %copy-start.46 = (f32[512]{0:T(512)}, f32[512]{0:T(512)S(1)}, u32[]{:S(2)}) copy-start(f32[512]{0:T(512)S(1)} %fusion.154) | copy-start | bytes 6148
  23.6 53.7 %copy-start.42 = (f32[8,1,256]{2,1,0:T(1,128)}, f32[8,1,256]{2,1,0:T(1,128)S(1)}, u32[]{:S(2)}) copy-start(f32[8,1,256]{2,1,0:T(1,128)S(1)} %convert_element_type.205) | copy-start | bytes 24580
  25.4 55.0 %copy-start.20 = (f32[512,64]{0,1:T(8,128)}, f32[512,64]{0,1:T(8,128)S(1)}, u32[]{:S(2)}) copy-start(f32[512,64]{0,1:T(8,128)S(1)} %get-tuple-element.328) | copy-start | bytes 393220
  144.8 341.7 %all-gather.19.cloned.1.call-start = ((), (), s32[]{:S(2)}) async-start(), calls=%async_computation.11 | async-start | bytes 9437184 | tf_op jit(solution)/shard_map/all_gather | solution.py:46
  145.3 397.2 %all-gather.21.cloned.1.call-start = ((), (), s32[]{:S(2)}) async-start(), calls=%async_computation.12 | async-start | bytes 9437184 | tf_op jit(solution)/shard_map/all_gather | solution.py:47
  145.9 454.2 %all-gather.23.cloned.1.call-start = ((), (), s32[]{:S(2)}) async-start(), calls=%async_computation.13 | async-start | bytes 9437184 | tf_op jit(solution)/shard_map/all_gather | solution.py:48
  146.5 742.0 %all-gather.25.cloned.1.call-start = ((), (), s32[]{:S(2)}) async-start(), calls=%async_computation.25 | async-start | bytes 20971520 | tf_op jit(solution)/shard_map/all_gather | solution.py:57
  181.1 862.9 %all-reduce.6.cloned.1.call-start = ((), (), s32[]{:S(2)}) async-start(), calls=%async_computation.14 | async-start | bytes 8388608 | tf_op jit(solution)/shard_map/psum | solution.py:63
  632.3 521.3 %reduce-scatter.10.cloned.1.call-start = ((), (), s32[]{:S(2)}) async-start(), calls=%async_computation.15 | async-start | bytes 1310720 | tf_op jit(solution)/shard_map/reduce_scatter | solution.py:302
  1129.7 51.1 %reduce-scatter.12.cloned.1.call-start = ((), (), s32[]{:S(2)}) async-start(), calls=%async_computation.16 | async-start | bytes 1310720 | tf_op jit(solution)/shard_map/reduce_scatter | solution.py:303
  1130.3 212.0 %all-reduce.8.cloned.1.call-start = ((), (), s32[]{:S(2)}) async-start(), calls=%async_computation.17 | async-start | bytes 8388608 | tf_op jit(solution)/shard_map/psum | solution.py:63
  1187.1 442.3 %all-gather.27.cloned.1.call-start = ((), (), s32[]{:S(2)}) async-start(), calls=%async_computation.26 | async-start | bytes 20971520 | tf_op jit(solution)/shard_map/all_gather | solution.py:57
  1216.3 451.1 %reduce-scatter.16.cloned.1.call-start = ((), (), s32[]{:S(2)}) async-start(), calls=%async_computation.19 | async-start | bytes 1179648 | tf_op jit(solution)/shard_map/reduce_scatter | solution.py:330
  1220.2 486.8 %reduce-scatter.18.cloned.1.call-start = ((), (), s32[]{:S(2)}) async-start(), calls=%async_computation.20 | async-start | bytes 1179648 | tf_op jit(solution)/shard_map/reduce_scatter | solution.py:331
  1222.2 539.6 %reduce-scatter.20.cloned.1.call-start = ((), (), s32[]{:S(2)}) async-start(), calls=%async_computation.21 | async-start | bytes 4718592 | tf_op jit(solution)/shard_map/reduce_scatter | solution.py:332
  1227.9 588.9 %reduce-scatter.14.cloned.1.call-start = ((), (), s32[]{:S(2)}) async-start(), calls=%async_computation.18 | async-start | bytes 4718592 | tf_op jit(solution)/shard_map/reduce_scatter | solution.py:329
  1233.9 703.0 %reduce-scatter.26.cloned.1.call-start = ((), (), s32[]{:S(2)}) async-start(), calls=%async_computation.24 | async-start | bytes 18874368 | tf_op jit(solution)/shard_map/reduce_scatter | solution.py:335
  1248.5 808.5 %reduce-scatter.24.cloned.1.call-start = ((), (), s32[]{:S(2)}) async-start(), calls=%async_computation.23 | async-start | bytes 18874368 | tf_op jit(solution)/shard_map/reduce_scatter | solution.py:334
  1261.1 916.3 %reduce-scatter.22.cloned.1.call-start = ((), (), s32[]{:S(2)}) async-start(), calls=%async_computation.22 | async-start | bytes 18874368 | tf_op jit(solution)/shard_map/reduce_scatter | solution.py:333
  1274.8 71.0 %copy-start.48 = (f32[2048]{0:T(1024)S(1)}, f32[2048]{0:T(1024)}, u32[]{:S(2)}) copy-start(f32[2048]{0:T(1024)} %get-tuple-element.233) | copy-start | bytes 24580
  1274.8 96.9 %copy-start.50 = (f32[512]{0:T(512)S(1)}, f32[512]{0:T(512)}, u32[]{:S(2)}) copy-start(f32[512]{0:T(512)} %copy-done.49) | copy-start | bytes 6148
  (68 other events, 483.1 us)
Sparse Core Ops, SparseCore 0:
  9.9 31.1 all-gather.14
  43.0 31.8 all-gather.16
  144.9 287.3 all-gather.28
  434.0 52.4 all-gather.18
  488.2 54.2 all-gather.20
  544.2 55.8 all-gather.22
  601.7 286.7 all-gather.24
  890.8 153.1 all-reduce.5
  1129.8 23.7 reduce-scatter.9
  1155.9 24.7 reduce-scatter.11
  1187.3 154.9 all-reduce.7
  1343.7 285.7 all-gather.26
  1633.2 34.1 reduce-scatter.15
  1671.0 35.9 reduce-scatter.17
  1710.8 51.0 reduce-scatter.19
  1765.6 51.1 reduce-scatter.13
  1820.8 115.9 reduce-scatter.25
  1940.9 116.1 reduce-scatter.23
  2061.2 116.1 reduce-scatter.21
